TPU v7x, 32 devices: a whole 2x2x4 slice. The times are simulated.
32 devices in a mesh: batch: 4 (over y, core), pts: 8 (over z, x).
Axes of the slice: x: 2, y: 2, z: 4, core: 2. Of those that a mesh axis runs over, the one named last changes fastest.
Arguments:
- mesh_attributes: bfloat16 [32768, 512], P(('batch', 'pts')), parts along dimension 0, may hold values from -12 to 12
- occupied_vertices_tally: int32 [32], P(('batch', 'pts')), parts along dimension 0, may hold values from 512 to 1024, as said below
- vertex_content_matrix: bfloat16 [4, 512, 512], replicated, may hold values from -0.25 to 0.25
- vertex_partition_matrix: bfloat16 [4, 512, 512], replicated, may hold values from -0.25 to 0.25
- partition_affinity_matrix: bfloat16 [4, 8, 64, 64], replicated, may hold values from -0.75 to 0.75
- softmax_sharpness: float32 [4, 8], replicated, may hold values from 0.02 to 1
- partition_asking_matrix: bfloat16 [4, 64, 64], replicated, may hold values from -0.75 to 0.75
- partition_matching_matrix: bfloat16 [4, 64, 64], replicated, may hold values from -0.75 to 0.75
- partition_content_matrix: bfloat16 [4, 64, 64], replicated, may hold values from -0.75 to 0.75
- attention_result_matrix: bfloat16 [4, 512, 512], replicated, may hold values from -0.25 to 0.25
- widening_matrix: bfloat16 [4, 512, 512], replicated, may hold values from -0.25 to 0.25
- contracting_matrix: bfloat16 [4, 512, 512], replicated, may hold values from -0.25 to 0.25
Outputs:
- result: bfloat16 [32768, 512], P(('batch', 'pts')), parts along dimension 0
There are 4 independent parts, one for each index of `batch`. A program takes and returns all parts, laid end to end along the dimension named above; an argument that names none is the same for every part. Nothing has to cross between parts.
Inputs may be any that keep to these rules, and one draw needn't show every extreme that they name: `occupied_vertices_tally`: the shard of some index holds 1024 live points in every draw.
All inputs are finite; a program needn't handle non-finite values.
Results may differ from a plain program's by a relative error of at most 0.0055.
Values sent between devices are 32-bit elements; how exact they have to be, the bound alone decides.
A program may use at most 64 MiB of HBM per device.

v0:
```python
import jax
import jax.numpy as jnp
from jax import lax
from jax.sharding import PartitionSpec as P


def layer_norm(stream):
    average = jnp.mean(stream, axis=-1, keepdims=True)
    centred = stream - average
    variance = jnp.mean(centred * centred, axis=-1, keepdims=True)
    return centred * lax.rsqrt(variance + 1e-05)


def attend_slices(
    tokens, partition_asking_matrix, partition_matching_matrix, partition_content_matrix
):
    highest = lax.Precision.HIGHEST
    queries = jnp.einsum(
        "hgd,de->hge", tokens, partition_asking_matrix.astype(jnp.float32), precision=highest
    )
    key_rows = jnp.einsum(
        "hgd,de->hge", tokens, partition_matching_matrix.astype(jnp.float32), precision=highest
    )
    val_rows = jnp.einsum(
        "hgd,de->hge", tokens, partition_content_matrix.astype(jnp.float32), precision=highest
    )
    scores = jnp.einsum("hgd,hkd->hgk", queries, key_rows, precision=highest) * queries.shape[
        -1
    ] ** (-0.5)
    attn_probs = jax.nn.softmax(scores, axis=-1)
    return jnp.einsum("hgk,hkd->hgd", attn_probs, val_rows, precision=highest)


def slice_tokens(numerator, mass):
    numerator, mass = lax.psum((numerator, mass), "pts")
    return numerator / (mass + 1e-05)[:, :, None]


def per_device(
    mesh_attributes,
    occupied_vertices_tally,
    vertex_content_matrix,
    vertex_partition_matrix,
    partition_affinity_matrix,
    softmax_sharpness,
    partition_asking_matrix,
    partition_matching_matrix,
    partition_content_matrix,
    attention_result_matrix,
    widening_matrix,
    contracting_matrix,
):
    points = mesh_attributes.shape[0]
    head_count = partition_affinity_matrix.shape[1]
    head_dim = partition_affinity_matrix.shape[2]
    live_mask = (jnp.arange(points, dtype=jnp.int32) < occupied_vertices_tally[0]).astype(
        jnp.float32
    )
    stream = mesh_attributes.astype(jnp.float32)
    group_count = 1
    attenders_within_team = head_count // group_count
    for stacked_level_index in range(vertex_content_matrix.shape[0]):
        normed = layer_norm(stream).astype(jnp.bfloat16)
        values = jnp.dot(
            normed, vertex_content_matrix[stacked_level_index], preferred_element_type=jnp.float32
        ).astype(jnp.bfloat16)
        values = values.reshape(points, head_count, head_dim)
        slice_feats = jnp.dot(
            normed, vertex_partition_matrix[stacked_level_index], preferred_element_type=jnp.float32
        ).astype(jnp.bfloat16)
        slice_feats = slice_feats.reshape(points, head_count, head_dim)
        partition_raw_affinities = jnp.einsum(
            "phd,hdg->phg",
            slice_feats,
            partition_affinity_matrix[stacked_level_index, 0:attenders_within_team],
            preferred_element_type=jnp.float32,
        )
        partition_raw_affinities = (
            partition_raw_affinities
            / softmax_sharpness[stacked_level_index, 0:attenders_within_team][None, :, None]
        )
        weights = (
            jax.nn.softmax(partition_raw_affinities, axis=-1) * live_mask[:, None, None]
        ).astype(jnp.bfloat16)
        numerator = jnp.einsum("phg,phd->hgd", weights, values, preferred_element_type=jnp.float32)
        mass = jnp.sum(weights, axis=0, dtype=jnp.float32)
        tokens = slice_tokens(numerator, mass)
        attended = attend_slices(
            tokens,
            partition_asking_matrix[stacked_level_index],
            partition_matching_matrix[stacked_level_index],
            partition_content_matrix[stacked_level_index],
        ).astype(jnp.bfloat16)
        pieces = jnp.einsum("phg,hgd->phd", weights, attended, preferred_element_type=jnp.float32)
        spread = pieces.reshape(points, head_count * head_dim).astype(jnp.bfloat16)
        stream = stream + jnp.dot(
            spread, attention_result_matrix[stacked_level_index], preferred_element_type=jnp.float32
        )
        normed = layer_norm(stream).astype(jnp.bfloat16)
        hidden = jax.nn.gelu(
            jnp.dot(
                normed, widening_matrix[stacked_level_index], preferred_element_type=jnp.float32
            )
        ).astype(jnp.bfloat16)
        stream = stream + jnp.dot(
            hidden, contracting_matrix[stacked_level_index], preferred_element_type=jnp.float32
        )
    return (stream * live_mask[:, None]).astype(jnp.bfloat16)


def solution(mesh):
    placed = (
        P(("batch", "pts"), None),
        P(("batch", "pts")),
        P(),
        P(),
        P(),
        P(),
        P(),
        P(),
        P(),
        P(),
        P(),
        P(),
    )
    return jax.shard_map(
        per_device, mesh=mesh, in_specs=placed, out_specs=P(("batch", "pts"), None), check_vma=False
    )
```

profile of v0, /device:TPU:0, one launch (start us, length us, event | category | flops | bytes accessed | tf_op | source)
XLA Modules:
  0.0 388.6 jit_solution(10073177145408402647)
XLA Ops:
  7.2 1.5 copy.13
  9.3 1.8 convolution_convert_fusion.11
  11.6 3.0 fusion.219
  14.6 1.8 convolution_convert_fusion.10
  16.8 1.2 fusion.240
  18.1 23.4 %psum.57 = f32[8,64]{1,0:T(8,128)S(1)} all-reduce(f32[8,64]{1,0:T(8,128)S(1)} %get-tuple-element.11), channel_id=1, replica_groups=mesh['batch'=4,'pts'=8] {'pts'}, use_global_device_ids=true, to_apply=%region_6.0 | all-reduce | flops 512 | bytes 4096 | tf_op jit(solution)/shard_map/psum | solution.py:35
  41.5 50.6 %all-reduce.5.cloned.1.call-done = f32[8,64,64]{2,1,0:T(8,128)} async-done(((f32[8,64,64]{2,1,0:T(8,128)}), f32[8,64,64]{2,1,0:T(8,128)}) %all-reduce.5.cloned.1.call-update) | async-done | bytes 131088 | tf_op jit(solution)/shard_map/psum | solution.py:35
  92.2 1.4 fusion.188
  93.5 1.3 fusion.186
  96.8 1.8 fusion.221
  99.0 1.0 copy-done
  100.0 4.2 %fusion.222 = (f32[1024]{0:T(1024)S(1)}, f32[1024,512]{0,1:T(8,128)S(1)}) fusion(f32[1024,512]{0,1:T(8,128)} %copy-done, bf16[4,512,512]{2,1,0:T(8,128)(2,1)} %param.23, f32[1024]{0:T(1024)S(1)} %add_rsqrt_fusion.6, f32[1024]{0:T(1024)S(1)} %broadcast_multiply_fusion.6, bf16[4,512,512]{2,1,0:T(8,128)(2,1)} %param.22), kind=kOutput, calls=%fused_computation.297 | convolution fusion | flops 1081080832 | bytes 7352320 | tf_op jit(solution)/shard_map/dot_general | solution.py:105
  104.5 1.8 convolution_convert_fusion.9
  106.3 1.8 convolution_convert_fusion.8
  108.6 3.0 fusion.225
  112.0 1.2 fusion.241
  113.3 20.1 %psum.59 = f32[8,64]{1,0:T(8,128)S(1)} all-reduce(f32[8,64]{1,0:T(8,128)S(1)} %get-tuple-element.9), channel_id=1, replica_groups=mesh['batch'=4,'pts'=8] {'pts'}, use_global_device_ids=true, to_apply=%region_17.0 | all-reduce | flops 512 | bytes 4096 | tf_op jit(solution)/shard_map/psum | solution.py:35
  133.4 50.2 %all-reduce.7.cloned.1.call-done = f32[8,64,64]{2,1,0:T(8,128)} async-done(((f32[8,64,64]{2,1,0:T(8,128)}), f32[8,64,64]{2,1,0:T(8,128)}) %all-reduce.7.cloned.1.call-update) | async-done | bytes 131088 | tf_op jit(solution)/shard_map/psum | solution.py:35
  183.7 1.3 fusion.182
  185.0 1.3 fusion.180
  188.3 1.8 fusion.227
  190.5 1.0 copy-done.1
  191.5 4.2 %fusion.228 = (f32[1024]{0:T(1024)S(1)}, f32[1024,512]{0,1:T(8,128)S(1)}) fusion(f32[1024,512]{0,1:T(8,128)} %copy-done.1, bf16[4,512,512]{2,1,0:T(8,128)(2,1)} %param.23, f32[1024]{0:T(1024)S(1)} %add_rsqrt_fusion.4, f32[1024]{0:T(1024)S(1)} %broadcast_multiply_fusion.4, bf16[4,512,512]{2,1,0:T(8,128)(2,1)} %param.22), kind=kOutput, calls=%fused_computation.301 | convolution fusion | flops 1081080832 | bytes 7352320 | tf_op jit(solution)/shard_map/dot_general | solution.py:105
  196.0 1.8 convolution_convert_fusion.7
  197.8 1.8 convolution_convert_fusion.6
  199.6 1.4 convolution_divide_fusion.1
  201.0 3.0 fusion.231
  204.4 1.2 fusion.242
  205.7 20.1 %psum.61 = f32[8,64]{1,0:T(8,128)S(1)} all-reduce(f32[8,64]{1,0:T(8,128)S(1)} %get-tuple-element.7), channel_id=1, replica_groups=mesh['batch'=4,'pts'=8] {'pts'}, use_global_device_ids=true, to_apply=%region_28.0 | all-reduce | flops 512 | bytes 4096 | tf_op jit(solution)/shard_map/psum | solution.py:35
  225.9 50.2 %all-reduce.9.cloned.1.call-done = f32[8,64,64]{2,1,0:T(8,128)} async-done(((f32[8,64,64]{2,1,0:T(8,128)}), f32[8,64,64]{2,1,0:T(8,128)}) %all-reduce.9.cloned.1.call-update) | async-done | bytes 131088 | tf_op jit(solution)/shard_map/psum | solution.py:35
  276.1 1.4 fusion.176
  277.4 1.3 fusion.174
  280.7 1.8 fusion.233
  282.9 1.0 copy-done.2
  283.9 4.2 %fusion.234 = (f32[1024]{0:T(1024)S(1)}, f32[1024,512]{0,1:T(8,128)S(1)}) fusion(f32[1024,512]{0,1:T(8,128)} %copy-done.2, bf16[4,512,512]{2,1,0:T(8,128)(2,1)} %param.23, f32[1024]{0:T(1024)S(1)} %add_rsqrt_fusion.2, f32[1024]{0:T(1024)S(1)} %broadcast_multiply_fusion.2, bf16[4,512,512]{2,1,0:T(8,128)(2,1)} %param.22), kind=kOutput, calls=%fused_computation.305 | convolution fusion | flops 1081080832 | bytes 7352320 | tf_op jit(solution)/shard_map/dot_general | solution.py:105
  288.4 1.8 convolution_convert_fusion.5
  290.2 1.8 convolution_convert_fusion.4
  292.1 1.4 convolution_divide_fusion
  293.5 3.0 fusion.237
  296.8 1.2 fusion.243
  298.1 20.1 %psum.63 = f32[8,64]{1,0:T(8,128)S(1)} all-reduce(f32[8,64]{1,0:T(8,128)S(1)} %get-tuple-element.5), channel_id=1, replica_groups=mesh['batch'=4,'pts'=8] {'pts'}, use_global_device_ids=true, to_apply=%region_39.0 | all-reduce | flops 512 | bytes 4096 | tf_op jit(solution)/shard_map/psum | solution.py:35
  318.2 50.2 %all-reduce.11.cloned.1.call-done = f32[8,64,64]{2,1,0:T(8,128)} async-done(((f32[8,64,64]{2,1,0:T(8,128)}), f32[8,64,64]{2,1,0:T(8,128)}) %all-reduce.11.cloned.1.call-update) | async-done | bytes 131088 | tf_op jit(solution)/shard_map/psum | solution.py:35
  368.4 1.4 fusion.170
  369.8 1.3 fusion.168
  373.1 1.8 fusion.239
  374.9 1.3 copy-done.3
  376.6 4.2 %multiply_convert_fusion = bf16[1024,512]{0,1:T(8,128)(2,1)S(1)} fusion(f32[1024,512]{0,1:T(8,128)} %copy-done.3, f32[1024]{0:T(1024)S(1)} %fusion.202, f32[1024]{0:T(1024)S(1)} %add_rsqrt_fusion, f32[1024]{0:T(1024)S(1)} %broadcast_multiply_fusion, bf16[4,512,512]{2,1,0:T(8,128)(2,1)} %param.23, bf16[4,512,512]{2,1,0:T(8,128)(2,1)} %param.22), kind=kOutput, calls=%fused_computation.63 | convolution fusion | flops 1081606144 | bytes 6303744 | tf_op jit(solution)/shard_map/dot_general | solution.py:105
  380.8 1.3 copy.19
  (87 shorter events, 13.1 us)
Async XLA Ops:
  6.5 85.6 %all-reduce.5.cloned.1.call-start = ((), (), s32[]{:S(2)}) async-start(), calls=%async_computation | async-start | bytes 524288 | tf_op jit(solution)/shard_map/psum | solution.py:35
  7.2 2.0 copy-start.4
  9.2 1.9 copy-start.5
  16.8 75.4 %copy-start.10 = (bf16[4,64,64]{2,1,0:T(8,128)(2,1)S(1)}, bf16[4,64,64]{2,1,0:T(8,128)(2,1)}, u32[]{:S(2)}) copy-start(bf16[4,64,64]{2,1,0:T(8,128)(2,1)} %param.18) | copy-start | bytes 98308
  16.8 76.7 %copy-start.11 = (bf16[4,64,64]{2,1,0:T(8,128)(2,1)S(1)}, bf16[4,64,64]{2,1,0:T(8,128)(2,1)}, u32[]{:S(2)}) copy-start(bf16[4,64,64]{2,1,0:T(8,128)(2,1)} %param.19) | copy-start | bytes 98308
  18.0 77.4 %copy-start.12 = (bf16[4,64,64]{2,1,0:T(8,128)(2,1)S(1)}, bf16[4,64,64]{2,1,0:T(8,128)(2,1)}, u32[]{:S(2)}) copy-start(bf16[4,64,64]{2,1,0:T(8,128)(2,1)} %param.20) | copy-start | bytes 98308
  18.1 165.6 %all-reduce.7.cloned.1.call-start = ((), (), s32[]{:S(2)}) async-start(), calls=%async_computation.1 | async-start | bytes 524288 | tf_op jit(solution)/shard_map/psum | solution.py:35
  92.2 3.3 copy-start.6
  98.7 1.4 copy-start
  113.3 162.8 %all-reduce.9.cloned.1.call-start = ((), (), s32[]{:S(2)}) async-start(), calls=%async_computation.2 | async-start | bytes 524288 | tf_op jit(solution)/shard_map/psum | solution.py:35
  183.7 3.3 copy-start.7
  190.1 1.4 copy-start.1
  205.7 162.8 %all-reduce.11.cloned.1.call-start = ((), (), s32[]{:S(2)}) async-start(), calls=%async_computation.3 | async-start | bytes 524288 | tf_op jit(solution)/shard_map/psum | solution.py:35
  276.1 3.3 copy-start.8
  282.5 1.4 copy-start.2
  368.4 3.3 copy-start.9
  374.9 1.4 copy-start.3
Sparse Core Ops, SparseCore 0:
  18.2 73.9 all-reduce.4
  113.4 70.2 all-reduce.6
  205.8 70.2 all-reduce.8
  298.2 70.1 all-reduce.10
where the time goes:
time: 390 us; the launch traced here: 389 us
  waiting for transfers between devices  201 us (52%)
  blocking collectives  83.8 us (21%)
  matrix products  65.3 us (17%)
  other arithmetic  16.3 us (4%)
  between operations  14.4 us (4%)
  local copies, waits for them, and re-layouts  7.29 us (2%)
    psum x4, waiting for transfers between devices, slice_tokens(): numerator, mass = lax.psum((numerator, mass), 'pts')  201 us
    psum x4, blocking collectives, slice_tokens(): numerator, mass = lax.psum((numerator, mass), 'pts')  83.8 us
    dot_general x4, matrix products, per_device(): jnp.dot(hidden, contracting_matrix[stacked_level_index], preferred_elemen...  16.8 us
    sub x4, other arithmetic, per_device(): jax.nn.softmax(partition_raw_affinities, axis=-1) * live_mask[:, None, None]  12.1 us
  transfers between devices with their start and end apart: 4, of which 4 were waited for; matrix products, arithmetic and copies ran while one was open for 0% of the time, Pallas kernels for 0%

commit v1 on v0

v1 whole, which is shorter than its diff:
```python
import functools

import jax
import jax.numpy as jnp
from jax import lax
from jax.experimental import pallas as pl
from jax.experimental.pallas import tpu as pltpu
from jax.sharding import PartitionSpec as P

F32 = jnp.float32
BF16 = jnp.bfloat16
LOG2E = 1.4426950408889634
HIGHEST = lax.Precision.HIGHEST


def dot(a, b, ca=1, cb=0, precision=None):
    return lax.dot_general(
        a, b, (((ca,), (cb,)), ((), ())), preferred_element_type=F32, precision=precision
    )


def norm_columns(s):
    scale = 1.0 / s.shape[0]
    centred = s - jnp.sum(s, axis=0, keepdims=True) * scale
    variance = jnp.sum(centred * centred, axis=0, keepdims=True) * scale
    return (centred * lax.rsqrt(variance + 1e-05)).astype(BF16)


def gelu(x):
    inner = x * (0.7978845608028654 + (0.7978845608028654 * 0.044715) * (x * x))
    half = 0.5 * x
    return half + half * jnp.tanh(inner)


def kernel(
    n,
    chunk,
    tally_ref,
    sharp_ref,
    x_ref,
    aff_ref,
    ask_ref,
    match_ref,
    cont_ref,
    wv_hbm,
    wp_hbm,
    wo_hbm,
    ww_hbm,
    wc_hbm,
    out_ref,
    wv,
    wp,
    wo,
    ww,
    wc,
    stream,
    wts,
    vals,
    fold,
    wt,
    mt,
    rs_send,
    rs_recv,
    ag_send,
    ag_recv,
    w_sem,
    rs_ssem,
    rs_rsem,
    ag_ssem,
    ag_rsem,
):
    layers, heads, dh, groups = aff_ref.shape
    points, feats = x_ref.shape
    hg = heads * groups
    owners = min(n, heads)
    stride = n // owners
    hpo = heads // owners
    half = dh // 2
    me = lax.axis_index("pts")
    my_owner = me // stride
    is_owner = lax.rem(me, stride) == 0
    chunks = points // chunk

    copies = []
    for j, (src, dst) in enumerate(
        ((wp_hbm, wp), (wv_hbm, wv), (wo_hbm, wo), (ww_hbm, ww), (wc_hbm, wc))
    ):
        copies.append((src, dst, j))

    def weight_copy(j, l):
        src, dst, k = copies[j]
        return pltpu.make_async_copy(src.at[l], dst.at[l], w_sem.at[k, l])

    for l in range(layers):
        for j in range(5):
            weight_copy(j, l).start()

    barrier = pltpu.get_barrier_semaphore()
    for k in range(1, n):
        pl.semaphore_signal(
            barrier,
            inc=1,
            device_id={"pts": lax.rem(me + k, n)},
            device_id_type=pl.DeviceIdType.MESH,
        )
    pl.semaphore_wait(barrier, n - 1)

    tally = tally_ref[0]

    def live(c):
        at = lax.broadcasted_iota(jnp.int32, (1, chunk), 1) + c * chunk
        return at < tally

    def prepare(l):
        slot = lax.rem(l, 2)
        for j in range(5):
            weight_copy(j, l).wait()
        zero = jnp.zeros((groups, dh), BF16)
        for p in range(heads // 2):
            top = aff_ref[l, 2 * p].astype(F32).T.astype(BF16)
            low = aff_ref[l, 2 * p + 1].astype(F32).T.astype(BF16)
            pair = jnp.concatenate(
                [jnp.concatenate([top, zero], 1), jnp.concatenate([zero, low], 1)], 0
            )
            both = dot(pair, wp[l, :, 2 * p * dh : 2 * (p + 1) * dh], 1, 1)
            for i in range(2):
                h = 2 * p + i
                fold[h * groups : (h + 1) * groups, :] = (
                    both[i * groups : (i + 1) * groups] * (LOG2E / sharp_ref[l, h])
                ).astype(BF16)
        for j, w in enumerate((wv, wo, ww, wc)):
            wt[slot, j] = w[l].T
        mt[slot] = dot(
            match_ref[l].astype(F32), ask_ref[l].astype(F32), 1, 1, HIGHEST
        ) * (dh**-0.5)

    for c in range(chunks):
        at = slice(c * chunk, (c + 1) * chunk)
        stream[:, at] = x_ref[at, :].astype(F32).T
    for q in range(vals.shape[0]):
        vals[q, vals.shape[1] - 16 :, :] = jnp.ones((16, points), BF16)
    prepare(jnp.int32(0))

    quads = vals.shape[0]
    qh = heads // quads
    lane = lax.broadcasted_iota(jnp.int32, (half, 2 * groups), 1) < groups
    lane_mass = lax.broadcasted_iota(jnp.int32, (8, 2 * groups), 1) < groups

    def rs_copy(owner, source):
        return pltpu.make_async_remote_copy(
            src_ref=rs_send.at[pl.ds(owner * hpo, hpo)],
            dst_ref=rs_recv.at[source],
            send_sem=rs_ssem.at[owner],
            recv_sem=rs_rsem.at[source],
            device_id={"pts": owner * stride},
            device_id_type=pl.DeviceIdType.MESH,
        )

    def ag_copy(owner, target):
        return pltpu.make_async_remote_copy(
            src_ref=ag_send,
            dst_ref=ag_recv.at[pl.ds(owner * hpo, hpo)],
            send_sem=ag_ssem.at[target],
            recv_sem=ag_rsem.at[owner],
            device_id={"pts": target},
            device_id_type=pl.DeviceIdType.MESH,
        )

    def other_owners(body):
        for k in range(owners):
            owner = lax.rem(my_owner + k, owners)
            if stride == 1:
                if k:
                    body(owner)
            else:
                pl.when(owner * stride != me)(functools.partial(body, owner))

    def layer(l, carry):
        slot = lax.rem(l, 2)
        for c in range(chunks):
            at = slice(c * chunk, (c + 1) * chunk)
            normed = norm_columns(stream[:, at])
            logits = dot(fold[...], normed)
            keep = live(c)
            for h in range(heads):
                part = logits[h * groups : (h + 1) * groups]
                e = jnp.exp2(part - jnp.max(part, axis=0, keepdims=True))
                r = jnp.where(keep, 1.0 / jnp.sum(e, axis=0, keepdims=True), 0.0)
                wts[h * groups : (h + 1) * groups, at] = (e * r).astype(BF16)
            v = dot(wt[slot, 0], normed).astype(BF16)
            for q in range(quads):
                vals[q, : qh * dh, at] = v[q * qh * dh : (q + 1) * qh * dh]
        for q in range(quads):
            total = dot(vals[q], wts[q * qh * groups : (q + 1) * qh * groups, :], 1, 1)
            for i in range(qh):
                h = q * qh + i
                cols = slice((i // 2) * 2 * groups, (i // 2 + 1) * 2 * groups)
                top = total[i * dh : i * dh + half, cols]
                low = total[i * dh + half : (i + 1) * dh, cols]
                mass = total[qh * dh : qh * dh + 8, cols]
                turned = pltpu.roll(mass, groups, 1)
                if i % 2 == 0:
                    rs_send[h, :half] = jnp.where(lane, top, pltpu.roll(low, groups, 1))
                    rs_send[h, half:] = jnp.where(lane_mass, mass, turned)
                else:
                    rs_send[h, :half] = jnp.where(lane, pltpu.roll(top, groups, 1), low)
                    rs_send[h, half:] = jnp.where(lane_mass, turned, mass)
        other_owners(lambda owner: rs_copy(owner, me).start())

        @pl.when(l + 1 < layers)
        def _():
            prepare_next(l)

        def attend():
            for k in range(1, n):
                rs_copy(my_owner, lax.rem(me + k, n)).wait_recv()
            for i in range(hpo):
                acc = rs_send[my_owner * hpo + i]
                for k in range(1, n):
                    acc = acc + rs_recv[lax.rem(me + k, n), i]
                packed = acc[:half] / (acc[half : half + 1] + 1e-05)
                tokens = jnp.concatenate([packed[:, :groups], packed[:, groups:]], 0)
                u = dot(mt[slot], tokens, 1, 0, HIGHEST)
                v = dot(cont_ref[l].astype(F32).T, tokens, 1, 0, HIGHEST)
                scores = dot(tokens.T, u, 1, 0, HIGHEST)
                e = jnp.exp(scores - jnp.max(scores, axis=0, keepdims=True))
                probs = e / jnp.sum(e, axis=0, keepdims=True)
                att = dot(v, probs, 1, 0, HIGHEST)
                ag_send[i] = jnp.concatenate([att[:half], att[half:]], 1)
            for k in range(1, n):
                ag_copy(my_owner, lax.rem(me + k, n)).start()
            for i in range(hpo):
                ag_recv[my_owner * hpo + i] = ag_send[i]

        if stride == 1:
            attend()
        else:
            pl.when(is_owner)(attend)

        other_owners(lambda owner: ag_copy(owner, me).wait_recv())

        mixes = []
        zero = jnp.zeros((2 * dh, 2 * groups), BF16)
        for p in range(heads // 2):
            even = ag_recv[2 * p]
            odd = ag_recv[2 * p + 1]
            block = jnp.concatenate(
                [
                    jnp.where(lane, even, 0.0),
                    jnp.where(lane, pltpu.roll(even, groups, 1), 0.0),
                    jnp.where(lane, 0.0, pltpu.roll(odd, groups, 1)),
                    jnp.where(lane, 0.0, odd),
                ],
                0,
            ).astype(BF16)
            mixes.append(
                dot(wt[slot, 1, :, 2 * p * dh : 2 * (p + 1) * dh], block).astype(BF16)
            )
        mix = jnp.concatenate(mixes, 1)
        for c in range(chunks):
            at = slice(c * chunk, (c + 1) * chunk)
            s = stream[:, at] + dot(mix, wts[:, at])
            hidden = gelu(dot(wt[slot, 2], norm_columns(s))).astype(BF16)
            stream[:, at] = s + dot(wt[slot, 3], hidden)

        other_owners(lambda owner: rs_copy(owner, me).wait_send())

        def sent():
            for k in range(1, n):
                ag_copy(my_owner, lax.rem(me + k, n)).wait_send()

        if stride == 1:
            sent()
        else:
            pl.when(is_owner)(sent)
        return carry

    def prepare_next(l):
        prepare(l + 1)

    lax.fori_loop(0, layers, layer, 0)

    for c in range(chunks):
        at = slice(c * chunk, (c + 1) * chunk)
        out_ref[at, :] = jnp.where(live(c), stream[:, at], 0.0).T.astype(BF16)


def per_device(n, x, tally, wv, wp, aff, sharp, ask, match, cont, wo, ww, wc):
    points, feats = x.shape
    layers, heads, dh, groups = aff.shape
    owners = min(n, heads)
    hpo = heads // owners
    quads = max(1, heads // 4)
    chunk = min(points, 256)
    vmem = pl.BlockSpec(memory_space=pltpu.VMEM)
    smem = pl.BlockSpec(memory_space=pltpu.SMEM)
    hbm = pl.BlockSpec(memory_space=pl.ANY)
    dma = pltpu.SemaphoreType.DMA
    return pl.pallas_call(
        functools.partial(kernel, n, chunk),
        out_shape=jax.ShapeDtypeStruct((points, feats), BF16),
        in_specs=[smem, smem] + [vmem] * 5 + [hbm] * 5,
        out_specs=vmem,
        scratch_shapes=[
            pltpu.VMEM(wv.shape, BF16),
            pltpu.VMEM(wp.shape, BF16),
            pltpu.VMEM(wo.shape, BF16),
            pltpu.VMEM(ww.shape, BF16),
            pltpu.VMEM(wc.shape, BF16),
            pltpu.VMEM((feats, points), F32),
            pltpu.VMEM((heads * groups, points), BF16),
            pltpu.VMEM((quads, heads // quads * dh + 16, points), BF16),
            pltpu.VMEM((heads * groups, feats), BF16),
            pltpu.VMEM((2, 4) + wv.shape[1:], BF16),
            pltpu.VMEM((2, dh, dh), F32),
            pltpu.VMEM((heads, dh // 2 + 8, 2 * groups), F32),
            pltpu.VMEM((n, hpo, dh // 2 + 8, 2 * groups), F32),
            pltpu.VMEM((hpo, dh // 2, 2 * groups), F32),
            pltpu.VMEM((heads, dh // 2, 2 * groups), F32),
            dma((5, layers)),
            dma((owners,)),
            dma((n,)),
            dma((n,)),
            dma((owners,)),
        ],
        compiler_params=pltpu.CompilerParams(
            collective_id=0, has_side_effects=True, vmem_limit_bytes=60 * 1024 * 1024
        ),
    )(tally, sharp, x, aff, ask, match, cont, wv, wp, wo, ww, wc)


def solution(mesh):
    rows = P(("batch", "pts"), None)
    placed = (rows, P(("batch", "pts"))) + (P(),) * 10
    return jax.shard_map(
        functools.partial(per_device, mesh.shape["pts"]),
        mesh=mesh,
        in_specs=placed,
        out_specs=rows,
        check_vma=False,
    )
```

time: 390 us -> 79.2 us (0.20)
  waiting for transfers between devices: 201 us -> 0 us
  blocking collectives: 83.8 us -> 0 us
  Pallas kernels: 0 us -> 76.1 us
  matrix products: 65.3 us -> 0 us
  other arithmetic: 16.3 us -> 0 us
  between operations: 14.4 us -> 0.66 us
  local copies, waits for them, and re-layouts: 7.29 us -> 2.26 us
    psum x4 -> x0, waiting for transfers between devices: 201 us -> none  [slice_tokens(): numerator, mass = lax.psum((numerator, mass), 'pts')]
    psum x4 -> x0, blocking collectives: 83.8 us -> none  [slice_tokens(): numerator, mass = lax.psum((numerator, mass), 'pts')]
    pallas_call x0 -> x1, Pallas kernels: none -> 76.1 us  [per_device(): pl.pallas_call(functools.partial(kernel, n, chunk), out_shape=jax.ShapeDt...]
    dot_general x48 -> x0, matrix products: 65.3 us -> none  [the longest x4 16.8 us: per_device(): jnp.dot(hidden, contracting_matrix[stacked_level_index], preferred_elemen...]
    sub x4 -> x0, other arithmetic: 12.1 us -> none  [per_device(): jax.nn.softmax(partition_raw_affinities, axis=-1) * live_mask[:, None, None]]
    reduce_sum x17 -> x0, other arithmetic: 4.17 us -> none  [the longest x8 2.39 us: layer_norm(): variance = jnp.mean(centred * centred, axis=-1, keepdims=True)]
  transfers between devices with their start and end apart: 4 -> 0, of which waited for: 4 -> 0; matrix products, arithmetic and copies ran while one was open for 0% -> 0% of each run, Pallas kernels for 0% -> 0%
where the time goes in v1:
time: 79.2 us; the launch traced here: 79 us
  Pallas kernels  76.1 us (96%)
  local copies, waits for them, and re-layouts  2.26 us (3%)
    pallas_call x1, Pallas kernels, per_device(): pl.pallas_call(functools.partial(kernel, n, chunk), out_shape=jax.ShapeDt...  76.1 us
    unnamed x1, local copies, waits for them, and re-layouts  2.26 us

profile of v1, /device:TPU:0, one launch (start us, length us, event | category | flops | bytes accessed | tf_op | source)
XLA Modules:
  0.0 79.0 jit_solution(10783666489789963634)
XLA Ops:
  0.7 76.1 %shard_map.118 = bf16[1024,512]{1,0:T(8,128)(2,1)} custom-call(s32[1]{0:T(128)S(6)} %copy.14.tally_ref, f32[4,8]{1,0:T(4,128)} %sharp_ref.1, bf16[1024,512]{1,0:T(8,128)(2,1)} %x_ref.1, bf16[4,8,64,64]{3,2,1,0:T(8,128)(2,1)} %aff_ref.1, bf16[4,64,64]{2,1,0:T(8,128)(2,1)} %ask_ref.1, bf16[4,64,64]{2,1,0:T(8,128)(2,1)} %match_ref.1, ...), custom_call_target="tpu_custom_call" | custom-call | tf_op jit(solution)/shard_map/pallas_call | solution.py:299
  76.7 2.3 %copy.15 = bf16[1024,512]{1,0:T(8,128)(2,1)} copy(bf16[1024,512]{1,0:T(8,128)(2,1)} %shard_map.118) | data formatting | bytes 2097152

commit v2 on v1

--- a/solution.py
+++ b/solution.py
@@ -54,15 +54,18 @@
     ww,
     wc,
     stream,
+    normed,
     wts,
     vals,
-    fold,
+    comb,
     wt,
+    x_buf,
     mt,
     rs_send,
     rs_recv,
     ag_send,
     ag_recv,
+    x_sem,
     w_sem,
     rs_ssem,
     rs_rsem,
@@ -71,7 +74,6 @@
 ):
     layers, heads, dh, groups = aff_ref.shape
     points, feats = x_ref.shape
-    hg = heads * groups
     owners = min(n, heads)
     stride = n // owners
     hpo = heads // owners
@@ -91,9 +93,9 @@
         src, dst, k = copies[j]
         return pltpu.make_async_copy(src.at[l], dst.at[l], w_sem.at[k, l])
 
-    for l in range(layers):
-        for j in range(5):
-            weight_copy(j, l).start()
+    def x_copy(c):
+        rows = pl.ds(c * chunk, chunk)
+        return pltpu.make_async_copy(x_ref.at[rows], x_buf.at[rows], x_sem.at[c])
 
     barrier = pltpu.get_barrier_semaphore()
     for k in range(1, n):
@@ -103,7 +105,12 @@
             device_id={"pts": lax.rem(me + k, n)},
             device_id_type=pl.DeviceIdType.MESH,
         )
-    pl.semaphore_wait(barrier, n - 1)
+    for c in range(chunks):
+        x_copy(c).start()
+    for j in range(5):
+        weight_copy(j, 0).start()
+
+    offsets = sorted(range(1, n), key=lambda k: min(k, n - k))
 
     tally = tally_ref[0]
 
@@ -115,6 +122,12 @@
         slot = lax.rem(l, 2)
         for j in range(5):
             weight_copy(j, l).wait()
+
+        @pl.when(l + 1 < layers)
+        def _():
+            for j in range(5):
+                weight_copy(j, l + 1).start()
+
         zero = jnp.zeros((groups, dh), BF16)
         for p in range(heads // 2):
             top = aff_ref[l, 2 * p].astype(F32).T.astype(BF16)
@@ -125,31 +138,42 @@
             both = dot(pair, wp[l, :, 2 * p * dh : 2 * (p + 1) * dh], 1, 1)
             for i in range(2):
                 h = 2 * p + i
-                fold[h * groups : (h + 1) * groups, :] = (
+                row = (h % qh) * groups
+                comb[h // qh, row : row + groups, :] = (
                     both[i * groups : (i + 1) * groups] * (LOG2E / sharp_ref[l, h])
                 ).astype(BF16)
-        for j, w in enumerate((wv, wo, ww, wc)):
+        turned = wv[l].T
+        for q in range(quads):
+            comb[q, qh * groups :, :] = turned[q * qh * dh : (q + 1) * qh * dh]
+        for j, w in enumerate((wo, ww, wc)):
             wt[slot, j] = w[l].T
         mt[slot] = dot(
             match_ref[l].astype(F32), ask_ref[l].astype(F32), 1, 1, HIGHEST
         ) * (dh**-0.5)
 
-    for c in range(chunks):
-        at = slice(c * chunk, (c + 1) * chunk)
-        stream[:, at] = x_ref[at, :].astype(F32).T
-    for q in range(vals.shape[0]):
-        vals[q, vals.shape[1] - 16 :, :] = jnp.ones((16, points), BF16)
-    prepare(jnp.int32(0))
-
     quads = vals.shape[0]
     qh = heads // quads
+
+    def cols_of(c):
+        return slice(c * chunk, (c + 1) * chunk)
+
+    for q in range(quads):
+        vals[q, vals.shape[1] - 16 :, :] = jnp.ones((16, points), BF16)
+    for c in range(chunks):
+        x_copy(c).wait()
+        s = x_buf[cols_of(c), :].astype(F32).T
+        stream[:, cols_of(c)] = s
+        normed[:, cols_of(c)] = norm_columns(s)
+    prepare(jnp.int32(0))
+    pl.semaphore_wait(barrier, n - 1)
+
     lane = lax.broadcasted_iota(jnp.int32, (half, 2 * groups), 1) < groups
     lane_mass = lax.broadcasted_iota(jnp.int32, (8, 2 * groups), 1) < groups
 
     def rs_copy(owner, source):
         return pltpu.make_async_remote_copy(
-            src_ref=rs_send.at[pl.ds(owner * hpo, hpo)],
-            dst_ref=rs_recv.at[source],
+            src_ref=rs_send.at[pl.ds(owner * hpo, hpo), pl.ds(0, half + 1)],
+            dst_ref=rs_recv.at[source, pl.ds(0, hpo), pl.ds(0, half + 1)],
             send_sem=rs_ssem.at[owner],
             recv_sem=rs_rsem.at[source],
             device_id={"pts": owner * stride},
@@ -166,31 +190,35 @@
             device_id_type=pl.DeviceIdType.MESH,
         )
 
-    def other_owners(body):
-        for k in range(owners):
+    def other_owners(body, low=0, high=owners):
+        order = sorted(range(owners), key=lambda k: min(k, owners - k))
+        for k in order:
             owner = lax.rem(my_owner + k, owners)
-            if stride == 1:
-                if k:
-                    body(owner)
+            if stride == 1 and k == 0:
+                continue
+            if stride == 1 and (low, high) == (0, owners):
+                body(owner)
             else:
-                pl.when(owner * stride != me)(functools.partial(body, owner))
+                here = (owner >= low) & (owner < high) & (owner * stride != me)
+                pl.when(here)(functools.partial(body, owner))
 
     def layer(l, carry):
         slot = lax.rem(l, 2)
-        for c in range(chunks):
-            at = slice(c * chunk, (c + 1) * chunk)
-            normed = norm_columns(stream[:, at])
-            logits = dot(fold[...], normed)
+
+        def product(q, c):
+            return dot(comb[q], normed[:, cols_of(c)])
+
+        def weigh(q, c, prod):
             keep = live(c)
-            for h in range(heads):
-                part = logits[h * groups : (h + 1) * groups]
+            for i in range(qh):
+                part = prod[i * groups : (i + 1) * groups]
                 e = jnp.exp2(part - jnp.max(part, axis=0, keepdims=True))
                 r = jnp.where(keep, 1.0 / jnp.sum(e, axis=0, keepdims=True), 0.0)
-                wts[h * groups : (h + 1) * groups, at] = (e * r).astype(BF16)
-            v = dot(wt[slot, 0], normed).astype(BF16)
-            for q in range(quads):
-                vals[q, : qh * dh, at] = v[q * qh * dh : (q + 1) * qh * dh]
-        for q in range(quads):
+                row = (q * qh + i) * groups
+                wts[row : row + groups, cols_of(c)] = (e * r).astype(BF16)
+            vals[q, : qh * dh, cols_of(c)] = prod[qh * groups :].astype(BF16)
+
+        def reduce_quad(q):
             total = dot(vals[q], wts[q * qh * groups : (q + 1) * qh * groups, :], 1, 1)
             for i in range(qh):
                 h = q * qh + i
@@ -205,7 +233,20 @@
                 else:
                     rs_send[h, :half] = jnp.where(lane, pltpu.roll(top, groups, 1), low)
                     rs_send[h, half:] = jnp.where(lane_mass, turned, mass)
-        other_owners(lambda owner: rs_copy(owner, me).start())
+            other_owners(
+                lambda owner: rs_copy(owner, me).start(),
+                q * qh // hpo,
+                (q + 1) * qh // hpo,
+            )
+
+        for q in range(quads):
+            prod = product(q, 0)
+            for c in range(chunks):
+                later = product(q, c + 1) if c + 1 < chunks else None
+                weigh(q, c, prod)
+                prod = later
+            if qh % hpo == 0:
+                reduce_quad(q)
 
         @pl.when(l + 1 < layers)
         def _():
@@ -227,7 +268,7 @@
                 probs = e / jnp.sum(e, axis=0, keepdims=True)
                 att = dot(v, probs, 1, 0, HIGHEST)
                 ag_send[i] = jnp.concatenate([att[:half], att[half:]], 1)
-            for k in range(1, n):
+            for k in offsets:
                 ag_copy(my_owner, lax.rem(me + k, n)).start()
             for i in range(hpo):
                 ag_recv[my_owner * hpo + i] = ag_send[i]
@@ -254,14 +295,31 @@
                 0,
             ).astype(BF16)
             mixes.append(
-                dot(wt[slot, 1, :, 2 * p * dh : 2 * (p + 1) * dh], block).astype(BF16)
+                dot(wt[slot, 0, :, 2 * p * dh : 2 * (p + 1) * dh], block).astype(BF16)
             )
         mix = jnp.concatenate(mixes, 1)
-        for c in range(chunks):
-            at = slice(c * chunk, (c + 1) * chunk)
-            s = stream[:, at] + dot(mix, wts[:, at])
-            hidden = gelu(dot(wt[slot, 2], norm_columns(s))).astype(BF16)
-            stream[:, at] = s + dot(wt[slot, 3], hidden)
+        base, wide, hid = {}, {}, {}
+
+        def stage(name, c):
+            if not 0 <= c < chunks:
+                return
+            at = cols_of(c)
+            if name == "mix":
+                base[c] = stream[:, at] + dot(mix, wts[:, at])
+            elif name == "widen":
+                wide[c] = dot(wt[slot, 1], norm_columns(base[c]))
+            elif name == "gelu":
+                hid[c] = gelu(wide[c]).astype(BF16)
+            elif name == "contract":
+                s = base[c] + dot(wt[slot, 2], hid[c])
+                stream[:, at] = s
+                normed[:, at] = norm_columns(s)
+
+        for t in range(chunks + 3):
+            stage("mix", t)
+            stage("gelu", t - 2)
+            stage("widen", t - 1)
+            stage("contract", t - 2)
 
         other_owners(lambda owner: rs_copy(owner, me).wait_send())
 
@@ -299,7 +357,7 @@
     return pl.pallas_call(
         functools.partial(kernel, n, chunk),
         out_shape=jax.ShapeDtypeStruct((points, feats), BF16),
-        in_specs=[smem, smem] + [vmem] * 5 + [hbm] * 5,
+        in_specs=[smem, smem, hbm] + [vmem] * 4 + [hbm] * 5,
         out_specs=vmem,
         scratch_shapes=[
             pltpu.VMEM(wv.shape, BF16),
@@ -308,15 +366,18 @@
             pltpu.VMEM(ww.shape, BF16),
             pltpu.VMEM(wc.shape, BF16),
             pltpu.VMEM((feats, points), F32),
+            pltpu.VMEM((feats, points), BF16),
             pltpu.VMEM((heads * groups, points), BF16),
             pltpu.VMEM((quads, heads // quads * dh + 16, points), BF16),
-            pltpu.VMEM((heads * groups, feats), BF16),
-            pltpu.VMEM((2, 4) + wv.shape[1:], BF16),
+            pltpu.VMEM((quads, heads // quads * (groups + dh), feats), BF16),
+            pltpu.VMEM((2, 3) + wv.shape[1:], BF16),
+            pltpu.VMEM(x.shape, BF16),
             pltpu.VMEM((2, dh, dh), F32),
             pltpu.VMEM((heads, dh // 2 + 8, 2 * groups), F32),
             pltpu.VMEM((n, hpo, dh // 2 + 8, 2 * groups), F32),
             pltpu.VMEM((hpo, dh // 2, 2 * groups), F32),
             pltpu.VMEM((heads, dh // 2, 2 * groups), F32),
+            dma((points // chunk,)),
             dma((5, layers)),
             dma((owners,)),
             dma((n,)),

time: 79.2 us -> 74.7 us (0.943)
  Pallas kernels: 76.1 us -> 71.6 us
    pallas_call x1, Pallas kernels: 76.1 us -> 71.6 us  [per_device(): pl.pallas_call(functools.partial(kernel, n, chunk), out_shape=jax.ShapeDt...]
where the time goes in v2:
time: 74.7 us; the launch traced here: 74.5 us
  Pallas kernels  71.6 us (96%)
  local copies, waits for them, and re-layouts  2.26 us (3%)
    pallas_call x1, Pallas kernels, per_device(): pl.pallas_call(functools.partial(kernel, n, chunk), out_shape=jax.ShapeDt...  71.6 us
    unnamed x1, local copies, waits for them, and re-layouts  2.26 us

profile of v2, /device:TPU:0, one launch (start us, length us, event | category | flops | bytes accessed | tf_op | source)
XLA Modules:
  0.0 74.5 jit_solution(4443556314507296904)
XLA Ops:
  0.7 71.6 %shard_map.118 = bf16[1024,512]{1,0:T(8,128)(2,1)} custom-call(s32[1]{0:T(128)S(6)} %copy.14.tally_ref, f32[4,8]{1,0:T(4,128)} %sharp_ref.1, bf16[1024,512]{1,0:T(8,128)(2,1)} %x_ref.1, bf16[4,8,64,64]{3,2,1,0:T(8,128)(2,1)} %aff_ref.1, bf16[4,64,64]{2,1,0:T(8,128)(2,1)} %ask_ref.1, bf16[4,64,64]{2,1,0:T(8,128)(2,1)} %match_ref.1, ...), custom_call_target="tpu_custom_call" | custom-call | tf_op jit(solution)/shard_map/pallas_call | solution.py:357
  72.3 2.3 %copy.15 = bf16[1024,512]{1,0:T(8,128)(2,1)} copy(bf16[1024,512]{1,0:T(8,128)(2,1)} %shard_map.118) | data formatting | bytes 2097152

commit v3 on v2

--- a/solution.py
+++ b/solution.py
@@ -340,7 +340,7 @@
 
     for c in range(chunks):
         at = slice(c * chunk, (c + 1) * chunk)
-        out_ref[at, :] = jnp.where(live(c), stream[:, at], 0.0).T.astype(BF16)
+        out_ref[:, at] = jnp.where(live(c), stream[:, at], 0.0).astype(BF16)
 
 
 def per_device(n, x, tally, wv, wp, aff, sharp, ask, match, cont, wo, ww, wc):
@@ -354,9 +354,9 @@
     smem = pl.BlockSpec(memory_space=pltpu.SMEM)
     hbm = pl.BlockSpec(memory_space=pl.ANY)
     dma = pltpu.SemaphoreType.DMA
-    return pl.pallas_call(
+    turned = pl.pallas_call(
         functools.partial(kernel, n, chunk),
-        out_shape=jax.ShapeDtypeStruct((points, feats), BF16),
+        out_shape=jax.ShapeDtypeStruct((feats, points), BF16),
         in_specs=[smem, smem, hbm] + [vmem] * 4 + [hbm] * 5,
         out_specs=vmem,
         scratch_shapes=[
@@ -388,6 +388,7 @@
             collective_id=0, has_side_effects=True, vmem_limit_bytes=60 * 1024 * 1024
         ),
     )(tally, sharp, x, aff, ask, match, cont, wv, wp, wo, ww, wc)
+    return turned.T
 
 
 def solution(mesh):

time: 74.7 us -> 74.5 us (level)
    transpose x0 -> x1, local copies, waits for them, and re-layouts: none -> 2.28 us  [per_device(): return turned.T]
    unnamed x1 -> x0, local copies, waits for them, and re-layouts: 2.26 us -> none
where the time goes in v3:
time: 74.5 us; the launch traced here: 74.4 us
  Pallas kernels  71.4 us (96%)
  local copies, waits for them, and re-layouts  2.28 us (3%)
    pallas_call x1, Pallas kernels, per_device(): pl.pallas_call(functools.partial(kernel, n, chunk), out_shape=jax.ShapeDt...  71.4 us
    transpose x1, local copies, waits for them, and re-layouts, per_device(): return turned.T  2.28 us

profile of v3, /device:TPU:0, one launch (start us, length us, event | category | flops | bytes accessed | tf_op | source)
XLA Modules:
  0.0 74.4 jit_solution(17248825043731865890)
XLA Ops:
  0.7 71.4 %shard_map.118 = bf16[512,1024]{1,0:T(8,128)(2,1)} custom-call(s32[1]{0:T(128)S(6)} %copy.14.tally_ref, f32[4,8]{1,0:T(4,128)} %sharp_ref.1, bf16[1024,512]{1,0:T(8,128)(2,1)} %x_ref.1, bf16[4,8,64,64]{3,2,1,0:T(8,128)(2,1)} %aff_ref.1, bf16[4,64,64]{2,1,0:T(8,128)(2,1)} %ask_ref.1, bf16[4,64,64]{2,1,0:T(8,128)(2,1)} %match_ref.1, ...), custom_call_target="tpu_custom_call" | custom-call | tf_op jit(solution)/shard_map/pallas_call | solution.py:357
  72.1 2.3 %copy.13 = bf16[1024,512]{1,0:T(8,128)(2,1)} copy(bf16[1024,512]{0,1:T(8,128)(2,1)} %bitcast.1) | data formatting | bytes 2097152 | tf_op jit(solution)/shard_map/transpose | solution.py:391
